TPU v7x, 512 devices: a whole 4x4x16 slice. The times are simulated.
512 devices in a mesh: lat: 32 (over z, x_lo), lon: 16 (over y, x_hi, core).
Axes of the slice: x: 4 (x_hi: 2, x_lo: 2; x = x_hi * 2 + x_lo), y: 4, z: 16, core: 2. Of those that a mesh axis runs over, the one named last changes fastest.
Arguments:
- observed: float32 [4096, 8192], P(('lat', 'lon')), may hold values from -12 to 12
- gauged: int32 [4096, 8192], P('lat', 'lon'), may hold values from 0 to 1, as said below
Outputs:
- coarsest_coeffs: float32 [512, 1024], P('lat', 'lon')
- coarse_coeffs: float32 [1024, 2048], P('lat', 'lon')
- fine_coeffs: float32 [2048, 4096], P('lat', 'lon')
- finest_coeffs: float32 [4096, 8192], P('lat', 'lon')
- imputed: float32 [4096, 8192], P(('lat', 'lon'))
Inputs may be any that keep to these rules, and one draw needn't show every extreme that they name: 1 marks a gauged cell.
All inputs are finite; a program needn't handle non-finite values.
Results may differ from a plain program's by a relative error of at most 0.00029.
Values sent between devices are 32-bit elements; how exact they have to be, the bound alone decides.
A program may use at most 64 MiB of HBM per device.

v0:
```python
import math
import jax
import jax.numpy as jnp
from jax import lax
from jax.sharding import PartitionSpec as P

LEVELS = 4
ITERS = 2
highest = lax.Precision.HIGHEST
data_weight = 2.0
kappa_term = 5.0
level_scales = (0.02, 0.03, 0.05, 0.08)


def with_halo(x, sides, width):
    for axis, dim in sides:
        size, length = (lax.axis_size(axis), x.shape[dim])
        up = [(i, (i + 1) % size) for i in range(size - 1)]
        down = [(j, i) for i, j in up]
        last = lax.slice_in_dim(x, length - width, length, axis=dim)
        first = lax.slice_in_dim(x, 0, width, axis=dim)
        before = lax.ppermute(last, axis, up)
        after = lax.ppermute(first, axis, down)
        x = jnp.concatenate([before, x, after], axis=dim)
    return x


def wendland(distance):
    remain = jnp.maximum(1.0 - distance, 0.0)
    return remain**6 * (35.0 * distance * distance + 18.0 * distance + 3.0) / 3.0


def basis_table(cell_total, node_total, spacing, cell_margin, node_margin):
    shape_full = (cell_total + 2 * cell_margin, node_total + 2 * node_margin)
    cell_idx = lax.broadcasted_iota(jnp.int32, shape_full, 0) - cell_margin
    node_idx = lax.broadcasted_iota(jnp.int32, shape_full, 1) - node_margin
    numerator = jnp.abs(2 * cell_idx - 2 * spacing * node_idx - (spacing - 1))
    return wendland(numerator.astype(jnp.float32) / (5.0 * spacing)) / math.sqrt(spacing)


def matmul(left, right):
    return jnp.dot(left, right, precision=highest, preferred_element_type=jnp.float32)


def stencil(values):
    beside = values[2:, 1:-1] + values[:-2, 1:-1] + values[1:-1, 2:] + values[1:-1, :-2]
    return kappa_term * values[1:-1, 1:-1] - beside


def level_products(first, second):
    accum = jnp.float32(0.0)
    for level_idx in range(len(first)):
        accum = accum + jnp.sum(first[level_idx] * second[level_idx])
    return accum


def norm_sum(residual):
    return lax.psum(level_products(residual, residual), ("lat", "lon"))


def body(observed, gauged):
    tiled = lax.all_to_all(observed, "lon", split_axis=1, concat_axis=0, tiled=True)
    lat_index = lax.axis_index("lat")
    lon_index = lax.axis_index("lon")
    lat_total = lax.axis_size("lat")
    lon_total = lax.axis_size("lon")
    rows_here, cols_here = gauged.shape
    gauge_float = gauged.astype(jnp.float32)
    spacings = [2 ** (LEVELS - 1 - level_idx) for level_idx in range(LEVELS)]
    node_shapes = [(rows_here // sp, cols_here // sp) for sp in spacings]
    fwd_lat = [basis_table(rows_here, node_shapes[k][0], spacings[k], 0, 2) for k in range(LEVELS)]
    fwd_lon = [basis_table(cols_here, node_shapes[k][1], spacings[k], 0, 2) for k in range(LEVELS)]
    valid_nodes = []
    for k in range(LEVELS):
        node_rows, node_cols = node_shapes[k]
        row_global = (
            lat_index * node_rows + lax.broadcasted_iota(jnp.int32, (node_rows + 2, 1), 0) - 1
        )
        col_global = (
            lon_index * node_cols + lax.broadcasted_iota(jnp.int32, (1, node_cols + 2), 1) - 1
        )
        row_valid = (row_global >= 0) & (row_global < node_rows * lat_total)
        col_valid = (col_global >= 0) & (col_global < node_cols * lon_total)
        valid_nodes.append((row_valid & col_valid).astype(jnp.float32))

    def synthesize(coeffs):
        surface = jnp.zeros((rows_here, cols_here), jnp.float32)
        extended_all = []
        for k in range(LEVELS):
            extended = with_halo(coeffs[k], (("lat", 0), ("lon", 1)), 2)
            surface = surface + matmul(matmul(fwd_lat[k], extended), fwd_lon[k].T)
            extended_all.append(extended)
        return (surface, extended_all)

    def adjoint(misfit):
        result = []
        widened = with_halo(misfit, (("lat", 0), ("lon", 1)), 16)
        for k in range(LEVELS):
            back_lat = basis_table(rows_here, node_shapes[k][0], spacings[k], 16, 0).T
            back_lon = basis_table(cols_here, node_shapes[k][1], spacings[k], 16, 0)
            result.append(matmul(matmul(back_lat, widened), back_lon))
        return result

    right_side = adjoint(data_weight * gauge_float * tiled)
    solution = [jnp.zeros_like(piece) for piece in right_side]
    surface_sum = jnp.zeros((rows_here, cols_here), jnp.float32)
    residual = right_side
    search = right_side
    res_norm = norm_sum(residual)
    for iteration in range(ITERS):
        apply_surface, apply_extended_all = synthesize(search)
        backs = adjoint(data_weight * gauge_float * apply_surface)
        curv_local = data_weight * jnp.sum(gauge_float * apply_surface * apply_surface)
        images = []
        for apply_k in range(LEVELS):
            smoothed = stencil(apply_extended_all[apply_k]) * valid_nodes[apply_k]
            images.append(backs[apply_k] + level_scales[apply_k] * stencil(smoothed))
            own_part = smoothed[1:-1, 1:-1]
            curv_local = curv_local + level_scales[apply_k] * jnp.sum(own_part * own_part)
        images, surface, curv_local = (images, apply_surface, curv_local)
        curv_sum = lax.psum(curv_local, ("lat", "lon"))
        step_size = res_norm / curv_sum
        solution = [solution[k] + step_size * search[k] for k in range(LEVELS)]
        surface_sum = surface_sum + step_size * surface
        if iteration + 1 < ITERS:
            residual = [residual[k] - step_size * images[k] for k in range(LEVELS)]
            new_norm = norm_sum(residual)
            search = [residual[k] + new_norm / res_norm * search[k] for k in range(LEVELS)]
            res_norm = new_norm
    final_surface, unused_rims = synthesize(solution)
    swath_field = lax.all_to_all(final_surface, "lon", split_axis=0, concat_axis=1, tiled=True)
    return (solution[0], solution[1], solution[2], solution[3], swath_field)


def solution(mesh):
    placed = (P(("lat", "lon"), None), P("lat", "lon"))
    return jax.shard_map(
        body,
        mesh=mesh,
        in_specs=placed,
        out_specs=(
            P("lat", "lon"),
            P("lat", "lon"),
            P("lat", "lon"),
            P("lat", "lon"),
            P(("lat", "lon"), None),
        ),
        check_vma=False,
    )
```

profile of v0, /device:TPU:98, one launch (start us, length us, event | category | flops | bytes accessed | tf_op | source)
XLA Modules:
  0.0 623.4 jit_solution(1043832198746908045)
XLA Ops:
  0.6 6.3 %all-to-all-start = ((f32[8,16,512]{2,0,1:T(8,128)}), f32[8,16,512]{2,0,1:T(8,128)S(1)}, u32[]{:S(2)}, u32[]{:S(2)}) async-start(f32[8,16,512]{2,0,1:T(8,128)} %bitcast.39), calls=%async_computation | async-start | bytes 524288 | tf_op jit(solution)/shard_map/all_to_all | solution.py:62
  7.4 9.0 %all-to-all-done = f32[8,16,512]{2,0,1:T(8,128)S(1)} async-done(((f32[8,16,512]{2,0,1:T(8,128)}), f32[8,16,512]{2,0,1:T(8,128)S(1)}, u32[]{:S(2)}, u32[]{:S(2)}) %all-to-all-start) | async-done | bytes 262176 | tf_op jit(solution)/shard_map/all_to_all | solution.py:62
  16.5 3.3 collective-permute-start.1
  19.9 4.6 collective-permute-start
  35.5 5.7 collective-permute-start.4
  45.1 6.0 collective-permute-start.12
  64.4 5.8 collective-permute-start.8
  75.6 8.3 %collective-permute-start.10 = (f32[36,2]{1,0:T(8,128)S(1)}, f32[36,2]{1,0:T(8,128)S(1)}, u32[]{:S(2)}, u32[]{:S(2)}) collective-permute-start(f32[36,2]{1,0:T(8,128)S(1)} %get-tuple-element.54), channel_id=1, source_target_pairs={{0,1},{1,2},{2,3},{3,4},{4,5},{5,6},{6,7},{7,8},{8,9},{9,10},{10,1... | collective-permute-start | bytes 872 | tf_op jit(solution)/shard_map/ppermute | solution.py:22
  84.5 5.8 collective-permute-start.16
  92.3 6.1 collective-permute-start.14
  104.4 6.2 %collective-permute-start.18 = (f32[132,2]{1,0:T(8,128)S(1)}, f32[132,2]{1,0:T(8,128)S(1)}, u32[]{:S(2)}, u32[]{:S(2)}) collective-permute-start(f32[132,2]{1,0:T(8,128)S(1)} %get-tuple-element.20), channel_id=1, source_target_pairs={{0,1},{1,2},{2,3},{3,4},{4,5},{5,6},{6,7},{7,8},{8,9},{9,10},{10,1... | collective-permute-start | bytes 3176 | tf_op jit(solution)/shard_map/ppermute | solution.py:22
  117.5 6.0 collective-permute-start.20
  127.5 5.5 collective-permute-start.22
  133.1 109.8 %all-reduce = (f32[]{:T(128)}, f32[]{:T(128)}) all-reduce(f32[]{:T(128)S(6)} %add.627, f32[]{:T(128)S(6)} %add.678), channel_id=1, replica_groups=mesh['lat'=32,'lon'=16] {'lat','lon'}, use_global_device_ids=true, to_apply=%region_4.0 | all-reduce | flops 2 | bytes 16 | tf_op jit(solution)/shard_map/psum | solution.py:58
  255.2 102.0 %psum.30 = f32[]{:T(128)} all-reduce(f32[]{:T(128)S(6)} %add.697), channel_id=1, replica_groups=mesh['lat'=32,'lon'=16] {'lat','lon'}, use_global_device_ids=true, to_apply=%region_15.0 | all-reduce | flops 1 | bytes 8 | tf_op jit(solution)/shard_map/psum | solution.py:58
  361.3 5.3 collective-permute-start.32
  368.5 6.0 collective-permute-start.24
  381.0 6.0 collective-permute-start.28
  391.5 4.7 collective-permute-start.30
  397.6 5.8 collective-permute-start.36
  405.4 5.5 collective-permute-start.34
  416.8 5.8 collective-permute-start.38
  430.5 104.2 %psum.31 = f32[]{:T(128)} all-reduce(f32[]{:T(128)S(6)} %add.720), channel_id=1, replica_groups=mesh['lat'=32,'lon'=16] {'lat','lon'}, use_global_device_ids=true, to_apply=%region_21.0 | all-reduce | flops 1 | bytes 8 | tf_op jit(solution)/shard_map/psum | solution.py:121
  536.2 4.4 collective-permute-start.49
  540.6 3.5 collective-permute-start.48
  546.5 5.6 collective-permute-start.40
  558.6 6.0 collective-permute-start.44
  567.6 6.0 collective-permute-start.52
  575.0 4.0 collective-permute-start.46
  580.4 5.8 collective-permute-start.50
  590.3 6.2 collective-permute-start.54
  600.5 22.0 %all_to_all.38 = f32[16,8,512]{2,1,0:T(8,128)S(1)} all-to-all(f32[16,8,512]{2,1,0:T(8,128)S(1)} %fusion.7), channel_id=1, replica_groups=mesh['lat'=32,'lon'=16] {'lon'}, dimensions={0} | all-to-all | bytes 524288 | tf_op jit(solution)/shard_map/all_to_all | solution.py:131
  (237 shorter events, 107.8 us)
Async XLA Ops:
  0.6 15.8 %all-to-all-start = ((f32[8,16,512]{2,0,1:T(8,128)}), f32[8,16,512]{2,0,1:T(8,128)S(1)}, u32[]{:S(2)}, u32[]{:S(2)}) async-start(f32[8,16,512]{2,0,1:T(8,128)} %bitcast.39), calls=%async_computation | async-start | bytes 524288 | tf_op jit(solution)/shard_map/all_to_all | solution.py:62
  32.9 26.8 %collective-permute-start.5 = (f32[2,64]{1,0:T(2,128)S(1)}, f32[2,64]{1,0:T(2,128)S(1)}, u32[]{:S(2)}, u32[]{:S(2)}) collective-permute-start(f32[2,64]{1,0:T(2,128)S(1)} %get-tuple-element.76), channel_id=1, source_target_pairs={{16,0},{32,16},{48,32},{64,48},{80,64},{96,80},{112,96},{128,112},... | collective-permute-start | bytes 1544 | tf_op jit(solution)/shard_map/ppermute | solution.py:23
  35.5 24.2 %collective-permute-start.4 = (f32[2,64]{1,0:T(2,128)S(1)}, f32[2,64]{1,0:T(2,128)S(1)}, u32[]{:S(2)}, u32[]{:S(2)}) collective-permute-start(f32[2,64]{1,0:T(2,128)S(1)} %get-tuple-element.75), channel_id=1, source_target_pairs={{0,16},{16,32},{32,48},{48,64},{64,80},{80,96},{96,112},{112,128},... | collective-permute-start | bytes 1544 | tf_op jit(solution)/shard_map/ppermute | solution.py:22
  43.2 47.7 %collective-permute-start.13 = (f32[2,256]{1,0:T(2,128)S(1)}, f32[2,256]{1,0:T(2,128)S(1)}, u32[]{:S(2)}, u32[]{:S(2)}) collective-permute-start(f32[2,256]{1,0:T(2,128)S(1)} %get-tuple-element.46), channel_id=1, source_target_pairs={{16,0},{32,16},{48,32},{64,48},{80,64},{96,80},{112,96},{128,112},... | collective-permute-start | bytes 6152 | tf_op jit(solution)/shard_map/ppermute | solution.py:23
  45.1 45.8 %collective-permute-start.12 = (f32[2,256]{1,0:T(2,128)S(1)}, f32[2,256]{1,0:T(2,128)S(1)}, u32[]{:S(2)}, u32[]{:S(2)}) collective-permute-start(f32[2,256]{1,0:T(2,128)S(1)} %get-tuple-element.45), channel_id=1, source_target_pairs={{0,16},{16,32},{32,48},{48,64},{64,80},{80,96},{96,112},{112,128},... | collective-permute-start | bytes 6152 | tf_op jit(solution)/shard_map/ppermute | solution.py:22
  52.8 20.7 %collective-permute-start.9 = (f32[2,128]{1,0:T(2,128)S(1)}, f32[2,128]{1,0:T(2,128)S(1)}, u32[]{:S(2)}, u32[]{:S(2)}) collective-permute-start(f32[2,128]{1,0:T(2,128)S(1)} %get-tuple-element.61), channel_id=1, source_target_pairs={{16,0},{32,16},{48,32},{64,48},{80,64},{96,80},{112,96},{128,112},... | collective-permute-start | bytes 3080 | tf_op jit(solution)/shard_map/ppermute | solution.py:23
  64.4 9.1 %collective-permute-start.8 = (f32[2,128]{1,0:T(2,128)S(1)}, f32[2,128]{1,0:T(2,128)S(1)}, u32[]{:S(2)}, u32[]{:S(2)}) collective-permute-start(f32[2,128]{1,0:T(2,128)S(1)} %get-tuple-element.60), channel_id=1, source_target_pairs={{0,16},{16,32},{32,48},{48,64},{64,80},{80,96},{96,112},{112,128},... | collective-permute-start | bytes 3080 | tf_op jit(solution)/shard_map/ppermute | solution.py:22
  70.4 32.6 %collective-permute-start.17 = (f32[2,512]{1,0:T(2,128)S(1)}, f32[2,512]{1,0:T(2,128)S(1)}, u32[]{:S(2)}, u32[]{:S(2)}) collective-permute-start(f32[2,512]{1,0:T(2,128)S(1)} %get-tuple-element.29), channel_id=1, source_target_pairs={{16,0},{32,16},{48,32},{64,48},{80,64},{96,80},{112,96},{128,112},... | collective-permute-start | bytes 12296 | tf_op jit(solution)/shard_map/ppermute | solution.py:23
  73.6 10.9 %collective-permute-start.11 = (f32[36,2]{1,0:T(8,128)S(1)}, f32[36,2]{1,0:T(8,128)S(1)}, u32[]{:S(2)}, u32[]{:S(2)}) collective-permute-start(f32[36,2]{1,0:T(8,128)S(1)} %get-tuple-element.55), channel_id=1, source_target_pairs={{1,0},{2,1},{3,2},{4,3},{5,4},{6,5},{7,6},{8,7},{9,8},{10,9},{11,1... | collective-permute-start | bytes 872 | tf_op jit(solution)/shard_map/ppermute | solution.py:23
  75.6 14.7 %collective-permute-start.10 = (f32[36,2]{1,0:T(8,128)S(1)}, f32[36,2]{1,0:T(8,128)S(1)}, u32[]{:S(2)}, u32[]{:S(2)}) collective-permute-start(f32[36,2]{1,0:T(8,128)S(1)} %get-tuple-element.54), channel_id=1, source_target_pairs={{0,1},{1,2},{2,3},{3,4},{4,5},{5,6},{6,7},{7,8},{8,9},{9,10},{10,1... | collective-permute-start | bytes 872 | tf_op jit(solution)/shard_map/ppermute | solution.py:22
  84.5 18.5 %collective-permute-start.16 = (f32[2,512]{1,0:T(2,128)S(1)}, f32[2,512]{1,0:T(2,128)S(1)}, u32[]{:S(2)}, u32[]{:S(2)}) collective-permute-start(f32[2,512]{1,0:T(2,128)S(1)} %get-tuple-element.28), channel_id=1, source_target_pairs={{0,16},{16,32},{32,48},{48,64},{64,80},{80,96},{96,112},{112,128},... | collective-permute-start | bytes 12296 | tf_op jit(solution)/shard_map/ppermute | solution.py:22
  115.6 10.5 %collective-permute-start.21 = (f32[16,512]{1,0:T(8,128)S(1)}, f32[16,512]{1,0:T(8,128)S(1)}, u32[]{:S(2)}, u32[]{:S(2)}) collective-permute-start(f32[16,512]{1,0:T(8,128)S(1)} %get-tuple-element.27), channel_id=1, source_target_pairs={{16,0},{32,16},{48,32},{64,48},{80,64},{96,80},{112,96},{128,112},... | collective-permute-start | bytes 98312 | tf_op jit(solution)/shard_map/ppermute | solution.py:23
  126.2 118.1 %collective-permute-start.23 = (f32[160,16]{1,0:T(8,128)S(1)}, f32[160,16]{1,0:T(8,128)S(1)}, u32[]{:S(2)}, u32[]{:S(2)}) collective-permute-start(f32[160,16]{1,0:T(8,128)S(1)} %get-tuple-element.13), channel_id=1, source_target_pairs={{1,0},{2,1},{3,2},{4,3},{5,4},{6,5},{7,6},{8,7},{9,8},{10,9},{11,1... | collective-permute-start | bytes 30728 | tf_op jit(solution)/shard_map/ppermute | solution.py:23
  127.5 116.8 %collective-permute-start.22 = (f32[160,16]{1,0:T(8,128)S(1)}, f32[160,16]{1,0:T(8,128)S(1)}, u32[]{:S(2)}, u32[]{:S(2)}) collective-permute-start(f32[160,16]{1,0:T(8,128)S(1)} %get-tuple-element.12), channel_id=1, source_target_pairs={{0,1},{1,2},{2,3},{3,4},{4,5},{5,6},{6,7},{7,8},{8,9},{9,10},{10,1... | collective-permute-start | bytes 30728 | tf_op jit(solution)/shard_map/ppermute | solution.py:22
  358.6 45.4 %collective-permute-start.33 = (f32[2,256]{1,0:T(2,128)S(1)}, f32[2,256]{1,0:T(2,128)S(1)}, u32[]{:S(2)}, u32[]{:S(2)}) collective-permute-start(f32[2,256]{1,0:T(2,128)S(1)} %get-tuple-element.44), channel_id=1, source_target_pairs={{16,0},{32,16},{48,32},{64,48},{80,64},{96,80},{112,96},{128,112},... | collective-permute-start | bytes 6152 | tf_op jit(solution)/shard_map/ppermute | solution.py:23
  361.3 42.7 %collective-permute-start.32 = (f32[2,256]{1,0:T(2,128)S(1)}, f32[2,256]{1,0:T(2,128)S(1)}, u32[]{:S(2)}, u32[]{:S(2)}) collective-permute-start(f32[2,256]{1,0:T(2,128)S(1)} %get-tuple-element.43), channel_id=1, source_target_pairs={{0,16},{16,32},{32,48},{48,64},{64,80},{80,96},{96,112},{112,128},... | collective-permute-start | bytes 6152 | tf_op jit(solution)/shard_map/ppermute | solution.py:22
  366.6 10.0 %collective-permute-start.25 = (f32[2,64]{1,0:T(2,128)S(1)}, f32[2,64]{1,0:T(2,128)S(1)}, u32[]{:S(2)}, u32[]{:S(2)}) collective-permute-start(f32[2,64]{1,0:T(2,128)S(1)} %get-tuple-element.74), channel_id=1, source_target_pairs={{16,0},{32,16},{48,32},{64,48},{80,64},{96,80},{112,96},{128,112},... | collective-permute-start | bytes 1544 | tf_op jit(solution)/shard_map/ppermute | solution.py:23
  374.5 15.6 %collective-permute-start.29 = (f32[2,128]{1,0:T(2,128)S(1)}, f32[2,128]{1,0:T(2,128)S(1)}, u32[]{:S(2)}, u32[]{:S(2)}) collective-permute-start(f32[2,128]{1,0:T(2,128)S(1)} %get-tuple-element.59), channel_id=1, source_target_pairs={{16,0},{32,16},{48,32},{64,48},{80,64},{96,80},{112,96},{128,112},... | collective-permute-start | bytes 3080 | tf_op jit(solution)/shard_map/ppermute | solution.py:23
  377.9 9.1 %collective-permute-start.26 = (f32[20,2]{1,0:T(8,128)S(1)}, f32[20,2]{1,0:T(8,128)S(1)}, u32[]{:S(2)}, u32[]{:S(2)}) collective-permute-start(f32[20,2]{1,0:T(8,128)S(1)} %get-tuple-element.67), channel_id=1, source_target_pairs={{0,1},{1,2},{2,3},{3,4},{4,5},{5,6},{6,7},{7,8},{8,9},{9,10},{10,1... | collective-permute-start | bytes 488 | tf_op jit(solution)/shard_map/ppermute | solution.py:22
  381.0 9.1 %collective-permute-start.28 = (f32[2,128]{1,0:T(2,128)S(1)}, f32[2,128]{1,0:T(2,128)S(1)}, u32[]{:S(2)}, u32[]{:S(2)}) collective-permute-start(f32[2,128]{1,0:T(2,128)S(1)} %get-tuple-element.58), channel_id=1, source_target_pairs={{0,16},{16,32},{32,48},{48,64},{64,80},{80,96},{96,112},{112,128},... | collective-permute-start | bytes 3080 | tf_op jit(solution)/shard_map/ppermute | solution.py:22
  387.0 28.4 %collective-permute-start.37 = (f32[2,512]{1,0:T(2,128)S(1)}, f32[2,512]{1,0:T(2,128)S(1)}, u32[]{:S(2)}, u32[]{:S(2)}) collective-permute-start(f32[2,512]{1,0:T(2,128)S(1)} %get-tuple-element.25), channel_id=1, source_target_pairs={{16,0},{32,16},{48,32},{64,48},{80,64},{96,80},{112,96},{128,112},... | collective-permute-start | bytes 12296 | tf_op jit(solution)/shard_map/ppermute | solution.py:23
  391.5 11.8 %collective-permute-start.30 = (f32[36,2]{1,0:T(8,128)S(1)}, f32[36,2]{1,0:T(8,128)S(1)}, u32[]{:S(2)}, u32[]{:S(2)}) collective-permute-start(f32[36,2]{1,0:T(8,128)S(1)} %get-tuple-element.52), channel_id=1, source_target_pairs={{0,1},{1,2},{2,3},{3,4},{4,5},{5,6},{6,7},{7,8},{8,9},{9,10},{10,1... | collective-permute-start | bytes 872 | tf_op jit(solution)/shard_map/ppermute | solution.py:22
  397.6 17.8 %collective-permute-start.36 = (f32[2,512]{1,0:T(2,128)S(1)}, f32[2,512]{1,0:T(2,128)S(1)}, u32[]{:S(2)}, u32[]{:S(2)}) collective-permute-start(f32[2,512]{1,0:T(2,128)S(1)} %get-tuple-element.24), channel_id=1, source_target_pairs={{0,16},{16,32},{32,48},{48,64},{64,80},{80,96},{96,112},{112,128},... | collective-permute-start | bytes 12296 | tf_op jit(solution)/shard_map/ppermute | solution.py:22
  536.2 38.8 %collective-permute-start.49 = (f32[2,256]{1,0:T(2,128)S(1)}, f32[2,256]{1,0:T(2,128)S(1)}, u32[]{:S(2)}, u32[]{:S(2)}) collective-permute-start(f32[2,256]{1,0:T(2,128)S(1)} %get-tuple-element.42), channel_id=1, source_target_pairs={{16,0},{32,16},{48,32},{64,48},{80,64},{96,80},{112,96},{128,112},... | collective-permute-start | bytes 6152 | tf_op jit(solution)/shard_map/ppermute | solution.py:23
  540.6 38.4 %collective-permute-start.48 = (f32[2,256]{1,0:T(2,128)S(1)}, f32[2,256]{1,0:T(2,128)S(1)}, u32[]{:S(2)}, u32[]{:S(2)}) collective-permute-start(f32[2,256]{1,0:T(2,128)S(1)} %get-tuple-element.41), channel_id=1, source_target_pairs={{0,16},{16,32},{32,48},{48,64},{64,80},{80,96},{96,112},{112,128},... | collective-permute-start | bytes 6152 | tf_op jit(solution)/shard_map/ppermute | solution.py:22
  544.2 9.9 %collective-permute-start.41 = (f32[2,64]{1,0:T(2,128)S(1)}, f32[2,64]{1,0:T(2,128)S(1)}, u32[]{:S(2)}, u32[]{:S(2)}) collective-permute-start(f32[2,64]{1,0:T(2,128)S(1)} %get-tuple-element.72), channel_id=1, source_target_pairs={{16,0},{32,16},{48,32},{64,48},{80,64},{96,80},{112,96},{128,112},... | collective-permute-start | bytes 1544 | tf_op jit(solution)/shard_map/ppermute | solution.py:23
  552.2 15.4 %collective-permute-start.45 = (f32[2,128]{1,0:T(2,128)S(1)}, f32[2,128]{1,0:T(2,128)S(1)}, u32[]{:S(2)}, u32[]{:S(2)}) collective-permute-start(f32[2,128]{1,0:T(2,128)S(1)} %get-tuple-element.57), channel_id=1, source_target_pairs={{16,0},{32,16},{48,32},{64,48},{80,64},{96,80},{112,96},{128,112},... | collective-permute-start | bytes 3080 | tf_op jit(solution)/shard_map/ppermute | solution.py:23
  555.5 9.1 %collective-permute-start.42 = (f32[20,2]{1,0:T(8,128)S(1)}, f32[20,2]{1,0:T(8,128)S(1)}, u32[]{:S(2)}, u32[]{:S(2)}) collective-permute-start(f32[20,2]{1,0:T(8,128)S(1)} %get-tuple-element.62), channel_id=1, source_target_pairs={{0,1},{1,2},{2,3},{3,4},{4,5},{5,6},{6,7},{7,8},{8,9},{9,10},{10,1... | collective-permute-start | bytes 488 | tf_op jit(solution)/shard_map/ppermute | solution.py:22
  558.6 15.0 %collective-permute-start.44 = (f32[2,128]{1,0:T(2,128)S(1)}, f32[2,128]{1,0:T(2,128)S(1)}, u32[]{:S(2)}, u32[]{:S(2)}) collective-permute-start(f32[2,128]{1,0:T(2,128)S(1)} %get-tuple-element.56), channel_id=1, source_target_pairs={{0,16},{16,32},{32,48},{48,64},{64,80},{80,96},{96,112},{112,128},... | collective-permute-start | bytes 3080 | tf_op jit(solution)/shard_map/ppermute | solution.py:22
  564.6 24.3 %collective-permute-start.53 = (f32[2,512]{1,0:T(2,128)S(1)}, f32[2,512]{1,0:T(2,128)S(1)}, u32[]{:S(2)}, u32[]{:S(2)}) collective-permute-start(f32[2,512]{1,0:T(2,128)S(1)} %get-tuple-element.23), channel_id=1, source_target_pairs={{16,0},{32,16},{48,32},{64,48},{80,64},{96,80},{112,96},{128,112},... | collective-permute-start | bytes 12296 | tf_op jit(solution)/shard_map/ppermute | solution.py:23
  567.6 21.4 %collective-permute-start.52 = (f32[2,512]{1,0:T(2,128)S(1)}, f32[2,512]{1,0:T(2,128)S(1)}, u32[]{:S(2)}, u32[]{:S(2)}) collective-permute-start(f32[2,512]{1,0:T(2,128)S(1)} %get-tuple-element.22), channel_id=1, source_target_pairs={{0,16},{16,32},{32,48},{48,64},{64,80},{80,96},{96,112},{112,128},... | collective-permute-start | bytes 12296 | tf_op jit(solution)/shard_map/ppermute | solution.py:22
  575.0 11.2 %collective-permute-start.46 = (f32[36,2]{1,0:T(8,128)S(1)}, f32[36,2]{1,0:T(8,128)S(1)}, u32[]{:S(2)}, u32[]{:S(2)}) collective-permute-start(f32[36,2]{1,0:T(8,128)S(1)} %get-tuple-element.50), channel_id=1, source_target_pairs={{0,1},{1,2},{2,3},{3,4},{4,5},{5,6},{6,7},{7,8},{8,9},{9,10},{10,1... | collective-permute-start | bytes 872 | tf_op jit(solution)/shard_map/ppermute | solution.py:22
  (30 other events, 383.5 us)
where the time goes:
time: 633 us; the launch traced here: 623 us
  blocking collectives  338 us (53%)
  starting transfers between devices  205 us (32%)
  matrix products  38.8 us (6%)
  between operations  18.3 us (3%)
  waiting for transfers between devices  12.2 us (2%)
  other arithmetic  9.16 us (1%)
    psum x2, blocking collectives, norm_sum(): return lax.psum(level_products(residual, residual), ('lat', 'lon'))  212 us
    ppermute x28, starting transfers between devices, with_halo(): before = lax.ppermute(last, axis, up)  148 us
    psum x1, blocking collectives, body(): curv_sum = lax.psum(curv_local, ('lat', 'lon'))  104 us
    ppermute x28, starting transfers between devices, with_halo(): after = lax.ppermute(first, axis, down)  50.6 us
    dot_general x40, matrix products, matmul(): jnp.dot(left, right, precision=highest, preferred_element_type=jnp.float32)  38.8 us
    all_to_all x1, blocking collectives, body(): lax.all_to_all(final_surface, 'lon', split_axis=0, concat_axis=1, tiled=T...  22 us
  transfers between devices with their start and end apart: 57, of which 5 were waited for; matrix products, arithmetic and copies ran while one was open for 4% of the time, Pallas kernels for 0%

commit v1 on v0

--- a/solution.py
+++ b/solution.py
@@ -118,7 +118,8 @@
             own_part = smoothed[1:-1, 1:-1]
             curv_local = curv_local + level_scales[apply_k] * jnp.sum(own_part * own_part)
         images, surface, curv_local = (images, apply_surface, curv_local)
-        curv_sum = lax.psum(curv_local, ("lat", "lon"))
+        one_axis = lax.psum(curv_local, "lat")
+        curv_sum = lax.psum(one_axis, "lon")
         step_size = res_norm / curv_sum
         solution = [solution[k] + step_size * search[k] for k in range(LEVELS)]
         surface_sum = surface_sum + step_size * surface

time: 633 us -> 719 us (1.14)
  blocking collectives: 338 us -> 426 us
    psum x1 -> x4, blocking collectives: 104 us -> 193 us  [the longest x2 120 us: body(): one_axis = lax.psum(curv_local, 'lat')]
where the time goes in v1:
time: 719 us; the launch traced here: 709 us
  blocking collectives  426 us (59%)
  starting transfers between devices  203 us (28%)
  matrix products  38.8 us (5%)
  between operations  18.2 us (3%)
  waiting for transfers between devices  12.2 us (2%)
  other arithmetic  9.16 us (1%)
    psum x2, blocking collectives, norm_sum(): return lax.psum(level_products(residual, residual), ('lat', 'lon'))  212 us
    ppermute x28, starting transfers between devices, with_halo(): before = lax.ppermute(last, axis, up)  147 us
    psum x2, blocking collectives, body(): one_axis = lax.psum(curv_local, 'lat')  120 us
    psum x2, blocking collectives, body(): curv_sum = lax.psum(one_axis, 'lon')  72.3 us
    ppermute x28, starting transfers between devices, with_halo(): after = lax.ppermute(first, axis, down)  49.3 us
    dot_general x40, matrix products, matmul(): jnp.dot(left, right, precision=highest, preferred_element_type=jnp.float32)  38.8 us
    all_to_all x1, blocking collectives, body(): lax.all_to_all(final_surface, 'lon', split_axis=0, concat_axis=1, tiled=T...  20.9 us
  transfers between devices with their start and end apart: 57, of which 5 were waited for; matrix products, arithmetic and copies ran while one was open for 4% of the time, Pallas kernels for 0%

profile of v1, /device:TPU:98, one launch (start us, length us, event | category | flops | bytes accessed | tf_op | source)
XLA Modules:
  0.0 709.0 jit_solution(6027871833750890899)
XLA Ops:
  0.6 6.3 all-to-all-start
  7.4 9.0 %all-to-all-done = f32[8,16,512]{2,0,1:T(8,128)S(1)} async-done(((f32[8,16,512]{2,0,1:T(8,128)}), f32[8,16,512]{2,0,1:T(8,128)S(1)}, u32[]{:S(2)}, u32[]{:S(2)}) %all-to-all-start) | async-done | bytes 262176 | tf_op jit(solution)/shard_map/all_to_all | solution.py:62
  19.9 4.6 collective-permute-start
  35.5 5.7 collective-permute-start.4
  45.1 6.0 collective-permute-start.12
  63.8 5.8 collective-permute-start.8
  74.9 8.3 %collective-permute-start.10 = (f32[36,2]{1,0:T(8,128)S(1)}, f32[36,2]{1,0:T(8,128)S(1)}, u32[]{:S(2)}, u32[]{:S(2)}) collective-permute-start(f32[36,2]{1,0:T(8,128)S(1)} %get-tuple-element.52), channel_id=1, source_target_pairs={{0,1},{1,2},{2,3},{3,4},{4,5},{5,6},{6,7},{7,8},{8,9},{9,10},{10,1... | collective-permute-start | bytes 872 | tf_op jit(solution)/shard_map/ppermute | solution.py:22
  83.9 5.8 collective-permute-start.16
  91.7 6.1 collective-permute-start.14
  103.7 6.2 collective-permute-start.18
  116.8 6.0 collective-permute-start.20
  126.1 60.2 %psum.43 = f32[]{:T(128)} all-reduce(f32[]{:T(128)S(6)} %add.682), channel_id=1, replica_groups=mesh['lat'=32,'lon'=16] {'lat'}, use_global_device_ids=true, to_apply=%region_10.0 | all-reduce | flops 1 | bytes 8 | tf_op jit(solution)/shard_map/psum | solution.py:121
  190.8 113.2 %psum.42 = f32[]{:T(128)} all-reduce(f32[]{:T(128)S(6)} %add.631), channel_id=1, replica_groups=mesh['lat'=32,'lon'=16] {'lat','lon'}, use_global_device_ids=true, to_apply=%region_4.0 | all-reduce | flops 1 | bytes 8 | tf_op jit(solution)/shard_map/psum | solution.py:58
  304.0 36.3 %psum.44 = f32[]{:T(128)} all-reduce(f32[]{:T(128)} %psum.43), channel_id=1, replica_groups=mesh['lat'=32,'lon'=16] {'lon'}, use_global_device_ids=true, to_apply=%region_11.0 | all-reduce | flops 1 | bytes 8 | tf_op jit(solution)/shard_map/psum | solution.py:122
  352.6 98.8 %psum.45 = f32[]{:T(128)} all-reduce(f32[]{:T(128)S(6)} %add.701), channel_id=1, replica_groups=mesh['lat'=32,'lon'=16] {'lat','lon'}, use_global_device_ids=true, to_apply=%region_16.0 | all-reduce | flops 1 | bytes 8 | tf_op jit(solution)/shard_map/psum | solution.py:58
  455.3 5.5 collective-permute-start.32
  462.7 6.0 collective-permute-start.24
  475.2 6.0 collective-permute-start.28
  485.9 4.5 collective-permute-start.30
  491.8 5.8 collective-permute-start.36
  499.6 5.5 collective-permute-start.34
  511.0 5.8 collective-permute-start.38
  524.7 60.2 %psum.46 = f32[]{:T(128)} all-reduce(f32[]{:T(128)S(6)} %add.724), channel_id=1, replica_groups=mesh['lat'=32,'lon'=16] {'lat'}, use_global_device_ids=true, to_apply=%region_22.0 | all-reduce | flops 1 | bytes 8 | tf_op jit(solution)/shard_map/psum | solution.py:121
  584.9 36.0 %psum.47 = f32[]{:T(128)} all-reduce(f32[]{:T(128)} %psum.46), channel_id=1, replica_groups=mesh['lat'=32,'lon'=16] {'lon'}, use_global_device_ids=true, to_apply=%region_23.0 | all-reduce | flops 1 | bytes 8 | tf_op jit(solution)/shard_map/psum | solution.py:122
  626.0 5.2 collective-permute-start.48
  633.2 6.0 collective-permute-start.40
  645.6 6.0 collective-permute-start.44
  654.6 6.0 collective-permute-start.52
  662.0 3.7 collective-permute-start.46
  667.1 5.8 collective-permute-start.50
  677.0 6.2 collective-permute-start.54
  687.2 20.9 %all_to_all.38 = f32[16,8,512]{2,1,0:T(8,128)S(1)} all-to-all(f32[16,8,512]{2,1,0:T(8,128)S(1)} %fusion.7), channel_id=1, replica_groups=mesh['lat'=32,'lon'=16] {'lon'}, dimensions={0} | all-to-all | bytes 524288 | tf_op jit(solution)/shard_map/all_to_all | solution.py:132
  (240 shorter events, 117.4 us)
Async XLA Ops:
  0.6 15.8 %all-to-all-start = ((f32[8,16,512]{2,0,1:T(8,128)}), f32[8,16,512]{2,0,1:T(8,128)S(1)}, u32[]{:S(2)}, u32[]{:S(2)}) async-start(f32[8,16,512]{2,0,1:T(8,128)} %bitcast.39), calls=%async_computation | async-start | bytes 524288 | tf_op jit(solution)/shard_map/all_to_all | solution.py:62
  32.9 26.1 %collective-permute-start.5 = (f32[2,64]{1,0:T(2,128)S(1)}, f32[2,64]{1,0:T(2,128)S(1)}, u32[]{:S(2)}, u32[]{:S(2)}) collective-permute-start(f32[2,64]{1,0:T(2,128)S(1)} %get-tuple-element.74), channel_id=1, source_target_pairs={{16,0},{32,16},{48,32},{64,48},{80,64},{96,80},{112,96},{128,112},... | collective-permute-start | bytes 1544 | tf_op jit(solution)/shard_map/ppermute | solution.py:23
  35.5 23.6 %collective-permute-start.4 = (f32[2,64]{1,0:T(2,128)S(1)}, f32[2,64]{1,0:T(2,128)S(1)}, u32[]{:S(2)}, u32[]{:S(2)}) collective-permute-start(f32[2,64]{1,0:T(2,128)S(1)} %get-tuple-element.73), channel_id=1, source_target_pairs={{0,16},{16,32},{32,48},{48,64},{64,80},{80,96},{96,112},{112,128},... | collective-permute-start | bytes 1544 | tf_op jit(solution)/shard_map/ppermute | solution.py:22
  43.2 47.0 %collective-permute-start.13 = (f32[2,256]{1,0:T(2,128)S(1)}, f32[2,256]{1,0:T(2,128)S(1)}, u32[]{:S(2)}, u32[]{:S(2)}) collective-permute-start(f32[2,256]{1,0:T(2,128)S(1)} %get-tuple-element.44), channel_id=1, source_target_pairs={{16,0},{32,16},{48,32},{64,48},{80,64},{96,80},{112,96},{128,112},... | collective-permute-start | bytes 6152 | tf_op jit(solution)/shard_map/ppermute | solution.py:23
  45.1 45.1 %collective-permute-start.12 = (f32[2,256]{1,0:T(2,128)S(1)}, f32[2,256]{1,0:T(2,128)S(1)}, u32[]{:S(2)}, u32[]{:S(2)}) collective-permute-start(f32[2,256]{1,0:T(2,128)S(1)} %get-tuple-element.43), channel_id=1, source_target_pairs={{0,16},{16,32},{32,48},{48,64},{64,80},{80,96},{96,112},{112,128},... | collective-permute-start | bytes 6152 | tf_op jit(solution)/shard_map/ppermute | solution.py:22
  52.8 20.0 %collective-permute-start.9 = (f32[2,128]{1,0:T(2,128)S(1)}, f32[2,128]{1,0:T(2,128)S(1)}, u32[]{:S(2)}, u32[]{:S(2)}) collective-permute-start(f32[2,128]{1,0:T(2,128)S(1)} %get-tuple-element.59), channel_id=1, source_target_pairs={{16,0},{32,16},{48,32},{64,48},{80,64},{96,80},{112,96},{128,112},... | collective-permute-start | bytes 3080 | tf_op jit(solution)/shard_map/ppermute | solution.py:23
  63.8 9.1 %collective-permute-start.8 = (f32[2,128]{1,0:T(2,128)S(1)}, f32[2,128]{1,0:T(2,128)S(1)}, u32[]{:S(2)}, u32[]{:S(2)}) collective-permute-start(f32[2,128]{1,0:T(2,128)S(1)} %get-tuple-element.58), channel_id=1, source_target_pairs={{0,16},{16,32},{32,48},{48,64},{64,80},{80,96},{96,112},{112,128},... | collective-permute-start | bytes 3080 | tf_op jit(solution)/shard_map/ppermute | solution.py:22
  69.7 32.6 %collective-permute-start.17 = (f32[2,512]{1,0:T(2,128)S(1)}, f32[2,512]{1,0:T(2,128)S(1)}, u32[]{:S(2)}, u32[]{:S(2)}) collective-permute-start(f32[2,512]{1,0:T(2,128)S(1)} %get-tuple-element.27), channel_id=1, source_target_pairs={{16,0},{32,16},{48,32},{64,48},{80,64},{96,80},{112,96},{128,112},... | collective-permute-start | bytes 12296 | tf_op jit(solution)/shard_map/ppermute | solution.py:23
  72.9 10.9 %collective-permute-start.11 = (f32[36,2]{1,0:T(8,128)S(1)}, f32[36,2]{1,0:T(8,128)S(1)}, u32[]{:S(2)}, u32[]{:S(2)}) collective-permute-start(f32[36,2]{1,0:T(8,128)S(1)} %get-tuple-element.53), channel_id=1, source_target_pairs={{1,0},{2,1},{3,2},{4,3},{5,4},{6,5},{7,6},{8,7},{9,8},{10,9},{11,1... | collective-permute-start | bytes 872 | tf_op jit(solution)/shard_map/ppermute | solution.py:23
  74.9 14.7 %collective-permute-start.10 = (f32[36,2]{1,0:T(8,128)S(1)}, f32[36,2]{1,0:T(8,128)S(1)}, u32[]{:S(2)}, u32[]{:S(2)}) collective-permute-start(f32[36,2]{1,0:T(8,128)S(1)} %get-tuple-element.52), channel_id=1, source_target_pairs={{0,1},{1,2},{2,3},{3,4},{4,5},{5,6},{6,7},{7,8},{8,9},{9,10},{10,1... | collective-permute-start | bytes 872 | tf_op jit(solution)/shard_map/ppermute | solution.py:22
  83.9 18.5 %collective-permute-start.16 = (f32[2,512]{1,0:T(2,128)S(1)}, f32[2,512]{1,0:T(2,128)S(1)}, u32[]{:S(2)}, u32[]{:S(2)}) collective-permute-start(f32[2,512]{1,0:T(2,128)S(1)} %get-tuple-element.26), channel_id=1, source_target_pairs={{0,16},{16,32},{32,48},{48,64},{64,80},{80,96},{96,112},{112,128},... | collective-permute-start | bytes 12296 | tf_op jit(solution)/shard_map/ppermute | solution.py:22
  114.9 71.3 %collective-permute-start.21 = (f32[16,512]{1,0:T(8,128)S(1)}, f32[16,512]{1,0:T(8,128)S(1)}, u32[]{:S(2)}, u32[]{:S(2)}) collective-permute-start(f32[16,512]{1,0:T(8,128)S(1)} %get-tuple-element.25), channel_id=1, source_target_pairs={{16,0},{32,16},{48,32},{64,48},{80,64},{96,80},{112,96},{128,112},... | collective-permute-start | bytes 98312 | tf_op jit(solution)/shard_map/ppermute | solution.py:23
  116.8 69.4 %collective-permute-start.20 = (f32[16,512]{1,0:T(8,128)S(1)}, f32[16,512]{1,0:T(8,128)S(1)}, u32[]{:S(2)}, u32[]{:S(2)}) collective-permute-start(f32[16,512]{1,0:T(8,128)S(1)} %get-tuple-element.24), channel_id=1, source_target_pairs={{0,16},{16,32},{32,48},{48,64},{64,80},{80,96},{96,112},{112,128},... | collective-permute-start | bytes 98312 | tf_op jit(solution)/shard_map/ppermute | solution.py:22
  186.3 155.3 %collective-permute-start.23 = (f32[160,16]{1,0:T(8,128)S(1)}, f32[160,16]{1,0:T(8,128)S(1)}, u32[]{:S(2)}, u32[]{:S(2)}) collective-permute-start(f32[160,16]{1,0:T(8,128)S(1)} %get-tuple-element.11), channel_id=1, source_target_pairs={{1,0},{2,1},{3,2},{4,3},{5,4},{6,5},{7,6},{8,7},{9,8},{10,9},{11,1... | collective-permute-start | bytes 30728 | tf_op jit(solution)/shard_map/ppermute | solution.py:23
  187.6 154.0 %collective-permute-start.22 = (f32[160,16]{1,0:T(8,128)S(1)}, f32[160,16]{1,0:T(8,128)S(1)}, u32[]{:S(2)}, u32[]{:S(2)}) collective-permute-start(f32[160,16]{1,0:T(8,128)S(1)} %get-tuple-element.10), channel_id=1, source_target_pairs={{0,1},{1,2},{2,3},{3,4},{4,5},{5,6},{6,7},{7,8},{8,9},{9,10},{10,1... | collective-permute-start | bytes 30728 | tf_op jit(solution)/shard_map/ppermute | solution.py:22
  452.8 45.4 %collective-permute-start.33 = (f32[2,256]{1,0:T(2,128)S(1)}, f32[2,256]{1,0:T(2,128)S(1)}, u32[]{:S(2)}, u32[]{:S(2)}) collective-permute-start(f32[2,256]{1,0:T(2,128)S(1)} %get-tuple-element.42), channel_id=1, source_target_pairs={{16,0},{32,16},{48,32},{64,48},{80,64},{96,80},{112,96},{128,112},... | collective-permute-start | bytes 6152 | tf_op jit(solution)/shard_map/ppermute | solution.py:23
  455.3 42.9 %collective-permute-start.32 = (f32[2,256]{1,0:T(2,128)S(1)}, f32[2,256]{1,0:T(2,128)S(1)}, u32[]{:S(2)}, u32[]{:S(2)}) collective-permute-start(f32[2,256]{1,0:T(2,128)S(1)} %get-tuple-element.41), channel_id=1, source_target_pairs={{0,16},{16,32},{32,48},{48,64},{64,80},{80,96},{96,112},{112,128},... | collective-permute-start | bytes 6152 | tf_op jit(solution)/shard_map/ppermute | solution.py:22
  460.8 10.0 %collective-permute-start.25 = (f32[2,64]{1,0:T(2,128)S(1)}, f32[2,64]{1,0:T(2,128)S(1)}, u32[]{:S(2)}, u32[]{:S(2)}) collective-permute-start(f32[2,64]{1,0:T(2,128)S(1)} %get-tuple-element.72), channel_id=1, source_target_pairs={{16,0},{32,16},{48,32},{64,48},{80,64},{96,80},{112,96},{128,112},... | collective-permute-start | bytes 1544 | tf_op jit(solution)/shard_map/ppermute | solution.py:23
  468.7 15.7 %collective-permute-start.29 = (f32[2,128]{1,0:T(2,128)S(1)}, f32[2,128]{1,0:T(2,128)S(1)}, u32[]{:S(2)}, u32[]{:S(2)}) collective-permute-start(f32[2,128]{1,0:T(2,128)S(1)} %get-tuple-element.57), channel_id=1, source_target_pairs={{16,0},{32,16},{48,32},{64,48},{80,64},{96,80},{112,96},{128,112},... | collective-permute-start | bytes 3080 | tf_op jit(solution)/shard_map/ppermute | solution.py:23
  472.1 9.1 %collective-permute-start.26 = (f32[20,2]{1,0:T(8,128)S(1)}, f32[20,2]{1,0:T(8,128)S(1)}, u32[]{:S(2)}, u32[]{:S(2)}) collective-permute-start(f32[20,2]{1,0:T(8,128)S(1)} %get-tuple-element.65), channel_id=1, source_target_pairs={{0,1},{1,2},{2,3},{3,4},{4,5},{5,6},{6,7},{7,8},{8,9},{9,10},{10,1... | collective-permute-start | bytes 488 | tf_op jit(solution)/shard_map/ppermute | solution.py:22
  475.2 9.3 %collective-permute-start.28 = (f32[2,128]{1,0:T(2,128)S(1)}, f32[2,128]{1,0:T(2,128)S(1)}, u32[]{:S(2)}, u32[]{:S(2)}) collective-permute-start(f32[2,128]{1,0:T(2,128)S(1)} %get-tuple-element.56), channel_id=1, source_target_pairs={{0,16},{16,32},{32,48},{48,64},{64,80},{80,96},{96,112},{112,128},... | collective-permute-start | bytes 3080 | tf_op jit(solution)/shard_map/ppermute | solution.py:22
  481.2 28.4 %collective-permute-start.37 = (f32[2,512]{1,0:T(2,128)S(1)}, f32[2,512]{1,0:T(2,128)S(1)}, u32[]{:S(2)}, u32[]{:S(2)}) collective-permute-start(f32[2,512]{1,0:T(2,128)S(1)} %get-tuple-element.23), channel_id=1, source_target_pairs={{16,0},{32,16},{48,32},{64,48},{80,64},{96,80},{112,96},{128,112},... | collective-permute-start | bytes 12296 | tf_op jit(solution)/shard_map/ppermute | solution.py:23
  485.9 11.7 %collective-permute-start.30 = (f32[36,2]{1,0:T(8,128)S(1)}, f32[36,2]{1,0:T(8,128)S(1)}, u32[]{:S(2)}, u32[]{:S(2)}) collective-permute-start(f32[36,2]{1,0:T(8,128)S(1)} %get-tuple-element.50), channel_id=1, source_target_pairs={{0,1},{1,2},{2,3},{3,4},{4,5},{5,6},{6,7},{7,8},{8,9},{9,10},{10,1... | collective-permute-start | bytes 872 | tf_op jit(solution)/shard_map/ppermute | solution.py:22
  491.8 17.8 %collective-permute-start.36 = (f32[2,512]{1,0:T(2,128)S(1)}, f32[2,512]{1,0:T(2,128)S(1)}, u32[]{:S(2)}, u32[]{:S(2)}) collective-permute-start(f32[2,512]{1,0:T(2,128)S(1)} %get-tuple-element.22), channel_id=1, source_target_pairs={{0,16},{16,32},{32,48},{48,64},{64,80},{80,96},{96,112},{112,128},... | collective-permute-start | bytes 12296 | tf_op jit(solution)/shard_map/ppermute | solution.py:22
  622.4 39.7 %collective-permute-start.49 = (f32[2,256]{1,0:T(2,128)S(1)}, f32[2,256]{1,0:T(2,128)S(1)}, u32[]{:S(2)}, u32[]{:S(2)}) collective-permute-start(f32[2,256]{1,0:T(2,128)S(1)} %get-tuple-element.40), channel_id=1, source_target_pairs={{16,0},{32,16},{48,32},{64,48},{80,64},{96,80},{112,96},{128,112},... | collective-permute-start | bytes 6152 | tf_op jit(solution)/shard_map/ppermute | solution.py:23
  626.0 39.7 %collective-permute-start.48 = (f32[2,256]{1,0:T(2,128)S(1)}, f32[2,256]{1,0:T(2,128)S(1)}, u32[]{:S(2)}, u32[]{:S(2)}) collective-permute-start(f32[2,256]{1,0:T(2,128)S(1)} %get-tuple-element.39), channel_id=1, source_target_pairs={{0,16},{16,32},{32,48},{48,64},{64,80},{80,96},{96,112},{112,128},... | collective-permute-start | bytes 6152 | tf_op jit(solution)/shard_map/ppermute | solution.py:22
  631.2 9.9 %collective-permute-start.41 = (f32[2,64]{1,0:T(2,128)S(1)}, f32[2,64]{1,0:T(2,128)S(1)}, u32[]{:S(2)}, u32[]{:S(2)}) collective-permute-start(f32[2,64]{1,0:T(2,128)S(1)} %get-tuple-element.70), channel_id=1, source_target_pairs={{16,0},{32,16},{48,32},{64,48},{80,64},{96,80},{112,96},{128,112},... | collective-permute-start | bytes 1544 | tf_op jit(solution)/shard_map/ppermute | solution.py:23
  639.2 15.4 %collective-permute-start.45 = (f32[2,128]{1,0:T(2,128)S(1)}, f32[2,128]{1,0:T(2,128)S(1)}, u32[]{:S(2)}, u32[]{:S(2)}) collective-permute-start(f32[2,128]{1,0:T(2,128)S(1)} %get-tuple-element.55), channel_id=1, source_target_pairs={{16,0},{32,16},{48,32},{64,48},{80,64},{96,80},{112,96},{128,112},... | collective-permute-start | bytes 3080 | tf_op jit(solution)/shard_map/ppermute | solution.py:23
  645.6 15.0 %collective-permute-start.44 = (f32[2,128]{1,0:T(2,128)S(1)}, f32[2,128]{1,0:T(2,128)S(1)}, u32[]{:S(2)}, u32[]{:S(2)}) collective-permute-start(f32[2,128]{1,0:T(2,128)S(1)} %get-tuple-element.54), channel_id=1, source_target_pairs={{0,16},{16,32},{32,48},{48,64},{64,80},{80,96},{96,112},{112,128},... | collective-permute-start | bytes 3080 | tf_op jit(solution)/shard_map/ppermute | solution.py:22
  651.7 24.0 %collective-permute-start.53 = (f32[2,512]{1,0:T(2,128)S(1)}, f32[2,512]{1,0:T(2,128)S(1)}, u32[]{:S(2)}, u32[]{:S(2)}) collective-permute-start(f32[2,512]{1,0:T(2,128)S(1)} %get-tuple-element.21), channel_id=1, source_target_pairs={{16,0},{32,16},{48,32},{64,48},{80,64},{96,80},{112,96},{128,112},... | collective-permute-start | bytes 12296 | tf_op jit(solution)/shard_map/ppermute | solution.py:23
  654.6 21.0 %collective-permute-start.52 = (f32[2,512]{1,0:T(2,128)S(1)}, f32[2,512]{1,0:T(2,128)S(1)}, u32[]{:S(2)}, u32[]{:S(2)}) collective-permute-start(f32[2,512]{1,0:T(2,128)S(1)} %get-tuple-element.20), channel_id=1, source_target_pairs={{0,16},{16,32},{32,48},{48,64},{64,80},{80,96},{96,112},{112,128},... | collective-permute-start | bytes 12296 | tf_op jit(solution)/shard_map/ppermute | solution.py:22
  662.0 10.9 %collective-permute-start.46 = (f32[36,2]{1,0:T(8,128)S(1)}, f32[36,2]{1,0:T(8,128)S(1)}, u32[]{:S(2)}, u32[]{:S(2)}) collective-permute-start(f32[36,2]{1,0:T(8,128)S(1)} %get-tuple-element.48), channel_id=1, source_target_pairs={{0,1},{1,2},{2,3},{3,4},{4,5},{5,6},{6,7},{7,8},{8,9},{9,10},{10,1... | collective-permute-start | bytes 872 | tf_op jit(solution)/shard_map/ppermute | solution.py:22
  (30 other events, 386.3 us)
